TPU v7x, 32 devices: a whole 2x2x4 slice. The times are simulated.
32 devices in a mesh: long: 8 (over y, x, core), short: 4 (over z).
Axes of the slice: x: 2, y: 2, z: 4, core: 2. Of those that a mesh axis runs over, the one named last changes fastest.
Arguments:
- transition: float32 [64, 384, 384], P(('long', 'short')), may hold values from 0 to 1
- innovation: float32 [64, 384], P(('long', 'short')), may hold values from 20 to 80
- observation: float32 [64, 384], P(('long', 'short')), may hold values from 0.05 to 0.5
- effects: float32 [64, 384, 384], P(('long', 'short')), may hold values from -0.0045 to 0.0045
- prior: float32 [384], replicated, may hold values from 0.5 to 2
- right_side: float32 [64, 384, 128], P(('long', 'short')), may hold values from -3 to 3
- tip_right: float32 [384, 128], replicated, may hold values from -6 to 6
Outputs:
- solution: float32 [64, 384, 128], P(('long', 'short'))
- tip_solution: float32 [384, 128], replicated
All inputs are finite; a program needn't handle non-finite values.
Results may differ from a plain program's by a relative error of at most 0.0003.
Values sent between devices are 32-bit elements; how exact they have to be, the bound alone decides.
A program may use at most 256 MiB of HBM per device.

v0:
```python
import functools

import jax
import jax.numpy as jnp
from jax import lax
from jax.experimental import pallas as pl
from jax.experimental.pallas import tpu as pltpu
from jax.sharding import PartitionSpec as P

AXES = ("long", "short")
PREC = lax.Precision.HIGHEST
LANES = 128
SUBLANES = 8
MESH = pl.DeviceIdType.MESH
F32 = jnp.float32


def dot(left, right):
    return jnp.dot(left, right, precision=PREC, preferred_element_type=F32)


def gram(left, right):
    return lax.dot_general(
        left, right, (((0,), (0,)), ((), ())), precision=PREC, preferred_element_type=F32
    )


def halve(x):
    high = x.astype(jnp.bfloat16)
    return high, (x - high.astype(F32)).astype(jnp.bfloat16)


def dot_three(left, right):
    high, low = halve(left)
    other_high, other_low = halve(right)
    return jnp.dot(
        jnp.concatenate([low, high, high], axis=1),
        jnp.concatenate([other_high, other_low, other_high], axis=0),
        preferred_element_type=F32,
    )


def gram_three(left, right):
    high, low = halve(left)
    other_high, other_low = halve(right)
    return lax.dot_general(
        jnp.concatenate([low, high, high], axis=0),
        jnp.concatenate([other_high, other_low, other_high], axis=0),
        (((0,), (0,)), ((), ())),
        preferred_element_type=F32,
    )


def inverse_two(a, b, c):
    inv = 1.0 / (a * c - b * b)
    return c * inv, -(b * inv), a * inv


def pivot_four(tiles, first, lane, sub):
    group, row = divmod(first, SUBLANES)
    shape = (SUBLANES, LANES)
    cols = [
        [jnp.broadcast_to(t[:, first + k : first + k + 1], shape) for t in tiles] for k in range(4)
    ]

    def entry(i, k):
        return cols[k][group][row + i : row + i + 1, :]

    a00, a01, a11 = inverse_two(entry(0, 0), entry(0, 1), entry(1, 1))
    b00, b01, b10, b11 = entry(0, 2), entry(0, 3), entry(1, 2), entry(1, 3)
    m00, m01 = a00 * b00 + a01 * b10, a00 * b01 + a01 * b11
    m10, m11 = a01 * b00 + a11 * b10, a01 * b01 + a11 * b11
    s00, s01, s11 = inverse_two(
        entry(2, 2) - (b00 * m00 + b10 * m10),
        entry(2, 3) - (b00 * m01 + b10 * m11),
        entry(3, 3) - (b01 * m01 + b11 * m11),
    )
    u00, u01 = m00 * s00 + m01 * s01, m00 * s01 + m01 * s11
    u10, u11 = m10 * s00 + m11 * s01, m10 * s01 + m11 * s11
    t01 = a01 + (u00 * m10 + u01 * m11)
    pivot_inverse = (
        (a00 + (u00 * m00 + u01 * m01), t01, -u00, -u01),
        (t01, a11 + (u10 * m10 + u11 * m11), -u10, -u11),
        (-u00, -u10, s00, s01),
        (-u01, -u11, s01, s11),
    )
    inside = jnp.logical_and(lane >= first, lane < first + 4)
    rows = [
        jnp.where(
            inside[:1],
            jnp.where(lane[:1] == first + k, 1.0, 0.0),
            tiles[group][row + k : row + k + 1, :],
        )
        for k in range(4)
    ]
    scaled = [
        jnp.broadcast_to(
            (p[0] * rows[0] + p[1] * rows[1]) + (p[2] * rows[2] + p[3] * rows[3]), shape
        )
        for p in pivot_inverse
    ]
    out = []
    for place, tile in enumerate(tiles):
        new = jnp.where(inside, 0.0, tile)
        for k in range(4):
            new = new - cols[k][place] * scaled[k]
        if place == group:
            for k in range(4):
                new = jnp.where(sub == row + k, scaled[k], new)
        out.append(new)
    return out


def pivot_inverse(block):
    lane = lax.broadcasted_iota(jnp.int32, (SUBLANES, LANES), 1)
    sub = lax.broadcasted_iota(jnp.int32, (SUBLANES, LANES), 0)
    tiles = [block[SUBLANES * g : SUBLANES * (g + 1), :] for g in range(LANES // SUBLANES)]
    for first in range(0, LANES, 4):
        tiles = pivot_four(tiles, first, lane, sub)
    return jnp.concatenate(tiles, axis=0)


def span(j):
    return pl.ds(j * LANES, LANES)


def sweep(w, slot, j, pivot):
    here = span(j)
    width = w.shape[1]
    columns = w[slot, :, here]
    w[slot, here, :] = dot(pivot, w[slot, here, :])
    w[slot, here, here] = pivot
    scaled = w[slot, here, :]
    w[slot, :, here] = jnp.zeros((width, LANES), F32)
    w[slot] = w[slot] - dot(columns, scaled)
    w[slot, here, :] = scaled


def next_pivot_block(w, slot, j, pivot):
    after = span(j + 1)
    scaled = dot(pivot, w[slot, span(j), after])
    return w[slot, after, after] - dot(w[slot, after, span(j)], scaled)


def host_side(segment):
    return 1 - lax.rem(segment, 2)


def host_of(level, segment):
    for _ in range(level):
        segment = 2 * segment + host_side(segment)
    return segment


def choose(values, index):
    picked = values[0]
    for k in range(1, len(values)):
        picked = jnp.where(index == k, values[k], picked)
    return picked


def column_of(row, width):
    turned = jnp.broadcast_to(row, (LANES, row.shape[1])).T
    return jnp.concatenate([turned] * (width // LANES), axis=1)


def diagonal(row):
    n = row.shape[1]
    at = lax.broadcasted_iota(jnp.int32, (n, n), 0)
    across = lax.broadcasted_iota(jnp.int32, (n, n), 1)
    return jnp.where(at == across, jnp.broadcast_to(row, (n, n)), 0.0)


def kernel(
    levels, shorts,
    trans, innov, observ, effects, prior, right, tip_right,
    out, tip_out,
    dd, ab, tip, work, abm, xs, ys,
    near_d, near_ab, far_d, far_ab, got_tip, sol, tip_sol, tip_rhs, base,
    send_sem, recv_sem, back_send, back_recv,
):
    n = trans.shape[1]
    k = effects.shape[2]
    m = right.shape[2]
    last = levels
    steps = n // LANES
    me = lax.axis_index("long") * shorts + lax.axis_index("short")

    segs = [me // (1 << v) for v in range(levels + 1)]
    halves = [lax.rem(s, 2) for s in segs]
    active = [host_of(v, segs[v]) == me for v in range(levels + 1)]
    partners = [host_of(v, segs[v] + 1 - 2 * halves[v]) for v in range(levels)]
    hosting = [active[v + 1] for v in range(levels)]
    sending = [jnp.logical_and(active[v], jnp.logical_not(active[v + 1])) for v in range(levels)]

    def place(position):
        return (position // shorts, lax.rem(position, shorts))

    barrier = pltpu.get_barrier_semaphore()
    for v in range(levels):
        @pl.when(active[v])
        def _():
            pl.semaphore_signal(barrier, inc=1, device_id=place(partners[v]), device_id_type=MESH)

    top = pl.ds(0, LANES)
    beyond = pl.ds(LANES, n - LANES)

    def forward_copy(what, v, near, far, target):
        src, dst = (
            lambda: (dd.at[near, top, top], near_d.at[v, top, top]),
            lambda: (dd.at[near, top, beyond], near_d.at[v, top, beyond]),
            lambda: (dd.at[near, beyond], near_d.at[v, beyond]),
            lambda: (xs.at[v + 1, far], xs.at[v + 1, far]),
            lambda: (ab.at[near], near_ab.at[v]),
            lambda: (dd.at[far], far_d.at[v]),
            lambda: (ab.at[far], far_ab.at[v]),
            lambda: (tip, got_tip.at[v]),
        )[what]()
        return pltpu.make_async_remote_copy(
            src_ref=src,
            dst_ref=dst,
            send_sem=send_sem.at[what],
            recv_sem=recv_sem.at[v, what],
            device_id=place(target),
            device_id_type=MESH,
        )

    first = jnp.where(me == 0, 0.0, 1.0).astype(F32)

    def weight(t, width):
        return column_of(innov[t : t + 1, :], width)

    work[0] = diagonal(innov[0:1, :] + observ[0:1, :]) + gram(trans[1], weight(1, n) * trans[1])

    count = active[0].astype(jnp.int32)
    for v in range(1, levels):
        count = count + active[v].astype(jnp.int32)
    pl.semaphore_wait(barrier, count)

    runs_at = [active[0]] + active + [active[last]]
    hosts_at = active + [active[last]] * 2

    def stage(s, carry):
        slot = lax.rem(s, 2)
        old = 1 - slot
        hosts = choose(hosts_at, s)
        merges = jnp.logical_and(hosts, jnp.logical_and(s > 0, s <= last))
        below = jnp.clip(s - 1, 0, last - 1)
        fs = jnp.clip(s - 1, 0, last)
        real = jnp.logical_and(s > 0, s <= last + 1)
        fed = jnp.logical_and(s > 1, s <= last + 1)
        fed_from = jnp.clip(fs - 1, 0, last - 1)
        inner = choose(halves, fs)
        outer = 1 - inner
        sent = jnp.logical_and(s > 0, choose(sending, below))
        sent = jnp.logical_and(sent, s <= last)
        sent_to = choose(partners, below)
        keep = jnp.where(real, jnp.where(fs == 0, last, fs - 1), last + 2)

        def send(what):
            @pl.when(sent)
            def _():
                forward_copy(what, below, outer, inner, sent_to).start()

        def arrived(what, v):
            forward_copy(what, v, 0, 1 - choose(halves, v), me).wait_recv()

        @pl.when(choose(runs_at, s))
        def _():
            near = 1 - choose(halves, below)

            @pl.when(merges)
            def _():
                arrived(0, below)
                work[slot, top, top] = dd[near, top, top] + near_d[below, top, top]

            @pl.when(s == last + 1)
            def _():
                work[slot] = dd[1]

            @pl.when(s == last + 2)
            def _():
                work[slot] = tip[:, :k] + diagonal(prior[...].reshape(1, k))
                tip_rhs[...] = tip[:, k:] + tip_right[...]

            @pl.when(fed)
            def _():
                arrived(3, fed_from)

            pivot = pivot_inverse(work[slot, top, top])
            y_in = dot(work[old], xs[fs, inner])
            ys[1] = y_in
            xs[fs + 1, inner] = -gram(xs[fs, outer], y_in)
            ys[2, top, top] = pivot
            send(3)

            @pl.when(fed)
            def _():
                arrived(4, fed_from)
                abm[...] = ab[inner] + near_ab[fed_from]
                arrived(5, fed_from)
                dd[inner] = far_d[fed_from]

            @pl.when(merges)
            def _():
                arrived(1, below)
                work[slot, top, beyond] = dd[near, top, beyond] + near_d[below, top, beyond]
                arrived(2, below)
                work[slot, beyond] = dd[near, beyond] + near_d[below, beyond]

            pivot = ys[2, top, top]
            block = next_pivot_block(work, slot, 0, pivot)
            sweep(work, slot, 0, pivot)
            ab[outer] = ab[outer] - gram_three(ys[0], abm[...])
            dd[inner] = dd[inner] - gram(xs[fs, inner], ys[1])
            ys[2, top, top] = pivot_inverse(block)
            send(4)
            send(5)

            @pl.when(fed)
            def _():
                arrived(6, fed_from)
                ab[inner] = far_ab[fed_from]

            for j in range(1, steps):
                pivot = ys[2, top, top]
                if j + 1 < steps:
                    block = next_pivot_block(work, slot, j, pivot)
                sweep(work, slot, j, pivot)
                if j == 1:
                    found = dot_three(work[old], abm[...])
                    near_ab[keep] = found
                    ab[inner] = ab[inner] - gram_three(ys[1], abm[...])
                    tip[...] = tip[...] - gram_three(abm[:, :k], found)
                if j + 1 < steps:
                    ys[2, top, top] = pivot_inverse(block)
                if j == 1:
                    send(6)

            @pl.when(real)
            def _():
                xs[fs, outer] = ys[0]
                xs[fs, inner] = ys[1]

            @pl.when(jnp.logical_or(sent, s == last + 1))
            def _():
                for v in range(levels):
                    @pl.when(jnp.logical_and(hosting[v], v < s))
                    def _():
                        forward_copy(7, v, 0, 1, me).wait_recv()
                        tip[...] = tip[...] + got_tip[v]

            send(7)

            @pl.when(jnp.logical_and(hosts, s <= last))
            def _():
                far = choose(halves, jnp.minimum(s, last))
                close = 1 - far

                @pl.when(s == 0)
                def _():
                    now = trans[0] * first
                    scaled = weight(0, n) * now
                    xs[0, 0] = -scaled
                    xs[0, 1] = -((weight(1, n) * trans[1]).T)
                    dd[0] = gram(now, scaled)
                    dd[1] = diagonal(innov[1:2, :] + observ[1:2, :])

                y_out = dot(work[slot], xs[s, close])
                ys[0] = y_out
                sends = jnp.logical_and(s < last, choose(sending, jnp.minimum(s, last - 1)))
                target = choose(partners, jnp.minimum(s, last - 1))
                level = jnp.minimum(s, last - 1)
                dd[close, top] = dd[close, top] - gram(xs[s, close, :, top], ys[0])

                @pl.when(sends)
                def _():
                    forward_copy(0, level, close, far, target).start()
                    forward_copy(1, level, close, far, target).start()

                dd[close, beyond] = dd[close, beyond] - gram(xs[s, close, :, beyond], ys[0])

                @pl.when(sends)
                def _():
                    forward_copy(2, level, close, far, target).start()

                @pl.when(s == 0)
                def _():
                    loaded_now = weight(0, k) * effects[0]
                    loaded_next = weight(1, k) * effects[1]
                    abm[:, :k] = gram_three(trans[1], loaded_next) - loaded_now
                    abm[:, k:] = right[0]
                    ab[0, :, :k] = gram_three(trans[0] * first, loaded_now)
                    ab[0, :, k:] = jnp.zeros((n, m), F32)
                    ab[1, :, :k] = -loaded_next
                    ab[1, :, k:] = right[1]
                    tip[:, :k] = gram_three(effects[0], loaded_now) + gram_three(effects[1], loaded_next)
                    tip[:, k:] = jnp.zeros((k, m), F32)

            @pl.when(s == last + 1)
            def _():
                found = dot_three(work[slot], ab[1])
                near_ab[last + 1] = found
                tip[...] = tip[...] - gram_three(ab[1, :, :k], found)

            @pl.when(s == last + 2)
            def _():
                found = dot_three(work[slot], tip_rhs[...])
                tip_sol[...] = found
                sol[levels, 1] = near_ab[last + 1, :, k:] - dot_three(near_ab[last + 1, :, :k], found)
                sol[levels, 0] = jnp.zeros((n, m), F32)

        return carry

    lax.fori_loop(0, levels + 3, stage, 0)

    def back_copy(what, v, half, target):
        other = 1 - half
        src = (tip_sol, sol.at[v + 1, other], sol.at[v, other])[what]
        dst = (tip_sol, sol.at[v, other], sol.at[v, half])[what]
        return pltpu.make_async_remote_copy(
            src_ref=src,
            dst_ref=dst,
            send_sem=back_send.at[v, what],
            recv_sem=back_recv.at[what],
            device_id=place(target),
            device_id_type=MESH,
        )

    def back(i, carry):
        v = levels - i
        half = choose(halves, v)
        waits = jnp.logical_and(v < levels, choose(sending + [sending[0]], v))
        hosts = jnp.logical_and(v < levels, choose(active[1:] + [active[levels]], v))
        level = jnp.minimum(v, levels - 1)
        lower = jnp.maximum(v - 1, 0)
        lower_half = choose(halves, lower)
        lower_target = choose(partners, lower)
        held = jnp.where(v == 0, levels, v - 1)

        @pl.when(choose(active, v))
        def _():
            @pl.when(waits)
            def _():
                back_copy(0, level, 1 - half, me).wait_recv()

            @pl.when(jnp.logical_or(waits, v == levels))
            def _():
                for w in reversed(range(levels)):
                    @pl.when(w < v)
                    def _():
                        back_copy(0, w, halves[w], partners[w]).start()

            base[...] = near_ab[held, :, k:] - dot_three(near_ab[held, :, :k], tip_sol[...])

            @pl.when(waits)
            def _():
                back_copy(1, level, 1 - half, me).wait_recv()

            @pl.when(hosts)
            def _():
                sol[level, half] = sol[level + 1, half]

            base[...] = base[...] - dot_three(xs[v, half], sol[v, half])

            @pl.when(waits)
            def _():
                back_copy(2, level, 1 - half, me).wait_recv()

            @pl.when(v > 0)
            def _():
                back_copy(1, lower, lower_half, lower_target).start()

            value = base[...] - dot_three(xs[v, 1 - half], sol[v, 1 - half])

            @pl.when(v > 0)
            def _():
                sol[lower, 1 - lower_half] = value
                back_copy(2, lower, lower_half, lower_target).start()

            @pl.when(v == 0)
            def _():
                out[0] = value

        return carry

    lax.fori_loop(0, levels + 1, back, 0)
    out[1] = sol[0, 1]
    tip_out[...] = tip_sol[...]

    for v in range(levels):
        @pl.when(sending[v])
        def _():
            for what in range(8):
                forward_copy(what, v, 1 - halves[v], halves[v], partners[v]).wait_send()

        @pl.when(hosting[v])
        def _():
            for what in range(3):
                back_copy(what, v, halves[v], partners[v]).wait_send()


def body(transition, innovation, observation, effects, prior, right_side, tip_right):
    blocks, n = innovation.shape
    k = prior.shape[0]
    m = right_side.shape[2]
    shorts = lax.axis_size("short")
    total = lax.axis_size(AXES)
    levels = total.bit_length() - 1
    assert blocks == 2 and total == 1 << levels
    vmem = pl.BlockSpec(memory_space=pltpu.VMEM)
    wide = k + m
    return pl.pallas_call(
        functools.partial(kernel, levels, shorts),
        out_shape=(
            jax.ShapeDtypeStruct(right_side.shape, F32),
            jax.ShapeDtypeStruct(tip_right.shape, F32),
        ),
        in_specs=[vmem] * 7,
        out_specs=(vmem, vmem),
        scratch_shapes=[
            pltpu.VMEM((2, n, n), F32),
            pltpu.VMEM((2, n, wide), F32),
            pltpu.VMEM((k, wide), F32),
            pltpu.VMEM((2, n, n), F32),
            pltpu.VMEM((n, wide), F32),
            pltpu.VMEM((levels + 2, 2, n, n), F32),
            pltpu.VMEM((3, n, n), F32),
            pltpu.VMEM((levels, n, n), F32),
            pltpu.VMEM((levels + 3, n, wide), F32),
            pltpu.VMEM((levels, n, n), F32),
            pltpu.VMEM((levels, n, wide), F32),
            pltpu.VMEM((levels, k, wide), F32),
            pltpu.VMEM((levels + 1, 2, n, m), F32),
            pltpu.VMEM((k, m), F32),
            pltpu.VMEM((k, m), F32),
            pltpu.VMEM((n, m), F32),
            pltpu.SemaphoreType.DMA((8,)),
            pltpu.SemaphoreType.DMA((levels, 8)),
            pltpu.SemaphoreType.DMA((levels, 3)),
            pltpu.SemaphoreType.DMA((3,)),
        ],
        compiler_params=pltpu.CompilerParams(
            collective_id=0, has_side_effects=True, vmem_limit_bytes=67000000
        ),
        name="arrow_solve",
    )(transition, innovation, observation, effects, prior, right_side, tip_right)


def solution(mesh):
    placed = (
        P(AXES, None, None),
        P(AXES, None),
        P(AXES, None),
        P(AXES, None, None),
        P(),
        P(AXES, None, None),
        P(),
    )
    return jax.shard_map(
        body,
        mesh=mesh,
        in_specs=placed,
        out_specs=(P(AXES, None, None), P()),
        check_vma=False,
    )
```

profile of v0, /device:TPU:0, one launch (start us, length us, event | category | flops | bytes accessed | tf_op | source)
XLA Modules:
  0.0 291.6 jit_solution(1771188040008063939)
XLA Ops:
  0.6 287.6 %arrow_solve.1 = (f32[2,384,128]{2,1,0:T(8,128)}, f32[384,128]{1,0:T(8,128)}) custom-call(f32[2,384,384]{2,1,0:T(8,128)} %trans.1, f32[2,384]{1,0:T(2,128)} %innov.1, f32[2,384]{1,0:T(2,128)} %observ.1, f32[2,384,384]{2,1,0:T(8,128)} %effects.1, f32[384]{0:T(512)} %prior.1, f32[2,384,128]{2,1,0:T(8,128)} %right.1, f32[384,128]{1,0:T(8,128)} %tip_right.1), custom_call_target="tpu_custom_call" | custom-call | tf_op jit(solution)/shard_map/arrow_solve/pallas_call | solution.py:513
  288.3 1.8 copy.11
  290.0 1.6 copy.12
where the time goes:
time: 292 us
  Pallas kernels  288 us (99%)
  local copies, waits for them, and re-layouts  3.38 us (1%)
    pallas_call x1, Pallas kernels, body(): pl.pallas_call(functools.partial(kernel, levels, shorts), out_shape=(jax....  288 us

commit v1 on v0

--- a/solution.py
+++ b/solution.py
@@ -128,27 +128,31 @@
     here = span(j)
     width = w.shape[1]
     columns = w[slot, :, here]
-    w[slot, here, :] = dot(pivot, w[slot, here, :])
+    w[slot, here, :] = dot_three(pivot, w[slot, here, :])
     w[slot, here, here] = pivot
     scaled = w[slot, here, :]
     w[slot, :, here] = jnp.zeros((width, LANES), F32)
-    w[slot] = w[slot] - dot(columns, scaled)
+    w[slot] = w[slot] - dot_three(columns, scaled)
     w[slot, here, :] = scaled
 
 
 def next_pivot_block(w, slot, j, pivot):
     after = span(j + 1)
-    scaled = dot(pivot, w[slot, span(j), after])
-    return w[slot, after, after] - dot(w[slot, after, span(j)], scaled)
-
-
-def host_side(segment):
+    scaled = dot_three(pivot, w[slot, span(j), after])
+    return w[slot, after, after] - dot_three(w[slot, after, span(j)], scaled)
+
+
+def host_side(level, segment):
+    if level == 0:
+        return 1 - lax.rem(segment // 2, 2)
+    if level == 1:
+        return lax.rem(segment, 2)
     return 1 - lax.rem(segment, 2)
 
 
 def host_of(level, segment):
-    for _ in range(level):
-        segment = 2 * segment + host_side(segment)
+    for low in reversed(range(level)):
+        segment = 2 * segment + host_side(low, segment)
     return segment
 
 
@@ -202,6 +206,9 @@
         def _():
             pl.semaphore_signal(barrier, inc=1, device_id=place(partners[v]), device_id_type=MESH)
 
+    twin = me + 4 * (1 - 2 * halves[2])
+    pl.semaphore_signal(barrier, inc=1, device_id=place(twin), device_id_type=MESH)
+
     top = pl.ds(0, LANES)
     beyond = pl.ds(LANES, n - LANES)
 
@@ -209,12 +216,13 @@
         src, dst = (
             lambda: (dd.at[near, top, top], near_d.at[v, top, top]),
             lambda: (dd.at[near, top, beyond], near_d.at[v, top, beyond]),
-            lambda: (dd.at[near, beyond], near_d.at[v, beyond]),
+            lambda: (dd.at[near, beyond, beyond], near_d.at[v, beyond, beyond]),
             lambda: (xs.at[v + 1, far], xs.at[v + 1, far]),
             lambda: (ab.at[near], near_ab.at[v]),
-            lambda: (dd.at[far], far_d.at[v]),
+            lambda: (dd.at[far, top], far_d.at[v, top]),
             lambda: (ab.at[far], far_ab.at[v]),
             lambda: (tip, got_tip.at[v]),
+            lambda: (dd.at[far, beyond, beyond], far_d.at[v, beyond, beyond]),
         )[what]()
         return pltpu.make_async_remote_copy(
             src_ref=src,
@@ -235,8 +243,9 @@
     count = active[0].astype(jnp.int32)
     for v in range(1, levels):
         count = count + active[v].astype(jnp.int32)
-    pl.semaphore_wait(barrier, count)
-
+    pl.semaphore_wait(barrier, count + 1)
+
+    crossed_at = [halves[0] < 0] + [halves[v + 1] == halves[v] for v in range(levels)]
     runs_at = [active[0]] + active + [active[last]]
     hosts_at = active + [active[last]] * 2
 
@@ -252,18 +261,28 @@
         fed_from = jnp.clip(fs - 1, 0, last - 1)
         inner = choose(halves, fs)
         outer = 1 - inner
+        crossed = choose(crossed_at, fs)
+        role = crossed.astype(jnp.int32)
+        mine = jnp.where(crossed, inner, outer)
+        other = 1 - mine
         sent = jnp.logical_and(s > 0, choose(sending, below))
         sent = jnp.logical_and(sent, s <= last)
         sent_to = choose(partners, below)
         keep = jnp.where(real, jnp.where(fs == 0, last, fs - 1), last + 2)
 
-        def send(what):
-            @pl.when(sent)
+        def send(what, also=True):
+            @pl.when(jnp.logical_and(sent, also))
             def _():
                 forward_copy(what, below, outer, inner, sent_to).start()
 
         def arrived(what, v):
             forward_copy(what, v, 0, 1 - choose(halves, v), me).wait_recv()
+
+        def take_far(side, v):
+            arrived(5, v)
+            arrived(8, v)
+            dd[side, top] = far_d[v, top]
+            dd[side, beyond, beyond] = far_d[v, beyond, beyond]
 
         @pl.when(choose(runs_at, s))
         def _():
@@ -276,14 +295,16 @@
 
             @pl.when(s == last + 1)
             def _():
-                work[slot] = dd[1]
+                work[slot, top] = dd[1, top]
+                work[slot, beyond, beyond] = dd[1, beyond, beyond]
+                work[slot, beyond, top] = dd[1, top, beyond].T
 
             @pl.when(s == last + 2)
             def _():
                 work[slot] = tip[:, :k] + diagonal(prior[...].reshape(1, k))
                 tip_rhs[...] = tip[:, k:] + tip_right[...]
 
-            @pl.when(fed)
+            @pl.when(jnp.logical_and(fed, jnp.logical_not(crossed)))
             def _():
                 arrived(3, fed_from)
 
@@ -297,30 +318,38 @@
             @pl.when(fed)
             def _():
                 arrived(4, fed_from)
-                abm[...] = ab[inner] + near_ab[fed_from]
-                arrived(5, fed_from)
-                dd[inner] = far_d[fed_from]
+                abm[...] = ab[other] + near_ab[fed_from]
+
+            @pl.when(jnp.logical_and(jnp.logical_and(fed, s <= last), jnp.logical_not(crossed)))
+            def _():
+                take_far(inner, fed_from)
 
             @pl.when(merges)
             def _():
                 arrived(1, below)
-                work[slot, top, beyond] = dd[near, top, beyond] + near_d[below, top, beyond]
+                edge = dd[near, top, beyond] + near_d[below, top, beyond]
+                work[slot, top, beyond] = edge
+                work[slot, beyond, top] = edge.T
                 arrived(2, below)
-                work[slot, beyond] = dd[near, beyond] + near_d[below, beyond]
+                work[slot, beyond, beyond] = dd[near, beyond, beyond] + near_d[below, beyond, beyond]
 
             pivot = ys[2, top, top]
             block = next_pivot_block(work, slot, 0, pivot)
             sweep(work, slot, 0, pivot)
-            ab[outer] = ab[outer] - gram_three(ys[0], abm[...])
-            dd[inner] = dd[inner] - gram(xs[fs, inner], ys[1])
+            ab[mine] = ab[mine] - gram_three(ys[role], abm[...])
+            dd[inner, top] = dd[inner, top] - gram(xs[fs, inner, :, top], ys[1])
+            dd[inner, beyond, beyond] = dd[inner, beyond, beyond] - gram(
+                xs[fs, inner, :, beyond], ys[1, :, beyond]
+            )
             ys[2, top, top] = pivot_inverse(block)
-            send(4)
-            send(5)
-
-            @pl.when(fed)
+            send(5, below < last - 1)
+            send(8, below < last - 1)
+            send(4, jnp.logical_not(crossed))
+
+            @pl.when(jnp.logical_and(fed, s <= last))
             def _():
                 arrived(6, fed_from)
-                ab[inner] = far_ab[fed_from]
+                ab[other] = far_ab[fed_from]
 
             for j in range(1, steps):
                 pivot = ys[2, top, top]
@@ -330,12 +359,13 @@
                 if j == 1:
                     found = dot_three(work[old], abm[...])
                     near_ab[keep] = found
-                    ab[inner] = ab[inner] - gram_three(ys[1], abm[...])
+                    ab[other] = ab[other] - gram_three(ys[1 - role], abm[...])
                     tip[...] = tip[...] - gram_three(abm[:, :k], found)
                 if j + 1 < steps:
                     ys[2, top, top] = pivot_inverse(block)
                 if j == 1:
-                    send(6)
+                    send(4, crossed)
+                    send(6, below < last - 1)
 
             @pl.when(real)
             def _():
@@ -350,7 +380,10 @@
                         forward_copy(7, v, 0, 1, me).wait_recv()
                         tip[...] = tip[...] + got_tip[v]
 
-            send(7)
+            @pl.when(sent)
+            def _():
+                to = jnp.where(below == 0, twin, sent_to)
+                forward_copy(7, below, outer, inner, to).start()
 
             @pl.when(jnp.logical_and(hosts, s <= last))
             def _():
@@ -366,6 +399,11 @@
                     dd[0] = gram(now, scaled)
                     dd[1] = diagonal(innov[1:2, :] + observ[1:2, :])
 
+                @pl.when(jnp.logical_and(s > 0, choose(crossed_at, jnp.minimum(s, last))))
+                def _():
+                    arrived(3, below)
+                    take_far(close, below)
+
                 y_out = dot(work[slot], xs[s, close])
                 ys[0] = y_out
                 sends = jnp.logical_and(s < last, choose(sending, jnp.minimum(s, last - 1)))
@@ -378,7 +416,9 @@
                     forward_copy(0, level, close, far, target).start()
                     forward_copy(1, level, close, far, target).start()
 
-                dd[close, beyond] = dd[close, beyond] - gram(xs[s, close, :, beyond], ys[0])
+                dd[close, beyond, beyond] = dd[close, beyond, beyond] - gram(
+                    xs[s, close, :, beyond], ys[0, :, beyond]
+                )
 
                 @pl.when(sends)
                 def _():
@@ -491,7 +531,7 @@
     for v in range(levels):
         @pl.when(sending[v])
         def _():
-            for what in range(8):
+            for what in (range(9) if v < levels - 1 else (0, 1, 2, 3, 4, 7)):
                 forward_copy(what, v, 1 - halves[v], halves[v], partners[v]).wait_send()
 
         @pl.when(hosting[v])
@@ -535,8 +575,8 @@
             pltpu.VMEM((k, m), F32),
             pltpu.VMEM((k, m), F32),
             pltpu.VMEM((n, m), F32),
-            pltpu.SemaphoreType.DMA((8,)),
-            pltpu.SemaphoreType.DMA((levels, 8)),
+            pltpu.SemaphoreType.DMA((9,)),
+            pltpu.SemaphoreType.DMA((levels, 9)),
             pltpu.SemaphoreType.DMA((levels, 3)),
             pltpu.SemaphoreType.DMA((3,)),
         ],

time: 292 us -> 263 us (0.901)
  the two profiles are of different devices: /device:TPU:0 before, /device:TPU:15 now
where the time goes in v1:
time: 263 us; the launch traced here: 258 us
  Pallas kernels  254 us (97%)
  local copies, waits for them, and re-layouts  3.38 us (1%)
    pallas_call x1, Pallas kernels, body(): pl.pallas_call(functools.partial(kernel, levels, shorts), out_shape=(jax....  254 us

profile of v1, /device:TPU:15, one launch (start us, length us, event | category | flops | bytes accessed | tf_op | source)
XLA Modules:
  0.0 258.1 jit_solution(4684300584061644656)
XLA Ops:
  0.6 254.1 %arrow_solve.1 = (f32[2,384,128]{2,1,0:T(8,128)}, f32[384,128]{1,0:T(8,128)}) custom-call(f32[2,384,384]{2,1,0:T(8,128)} %trans.1, f32[2,384]{1,0:T(2,128)} %innov.1, f32[2,384]{1,0:T(2,128)} %observ.1, f32[2,384,384]{2,1,0:T(8,128)} %effects.1, f32[384]{0:T(512)} %prior.1, f32[2,384,128]{2,1,0:T(8,128)} %right.1, f32[384,128]{1,0:T(8,128)} %tip_right.1), custom_call_target="tpu_custom_call" | custom-call | tf_op jit(solution)/shard_map/arrow_solve/pallas_call | solution.py:553
  254.7 1.8 copy.11
  256.5 1.6 copy.12

commit v2 on v1

--- a/solution.py
+++ b/solution.py
@@ -501,13 +501,19 @@
             def _():
                 sol[level, half] = sol[level + 1, half]
 
+            early = half == 1 - lower_half
+
+            @pl.when(jnp.logical_and(v > 0, early))
+            def _():
+                back_copy(1, lower, lower_half, lower_target).start()
+
             base[...] = base[...] - dot_three(xs[v, half], sol[v, half])
 
             @pl.when(waits)
             def _():
                 back_copy(2, level, 1 - half, me).wait_recv()
 
-            @pl.when(v > 0)
+            @pl.when(jnp.logical_and(v > 0, jnp.logical_not(early)))
             def _():
                 back_copy(1, lower, lower_half, lower_target).start()
 

time: 263 us -> 260 us (0.989)
  no operation moved by 1% of the time
where the time goes in v2:
time: 260 us; the launch traced here: 257 us
  Pallas kernels  253 us (97%)
  local copies, waits for them, and re-layouts  3.38 us (1%)
    pallas_call x1, Pallas kernels, body(): pl.pallas_call(functools.partial(kernel, levels, shorts), out_shape=(jax....  253 us

profile of v2, /device:TPU:15, one launch (start us, length us, event | category | flops | bytes accessed | tf_op | source)
XLA Modules:
  0.0 256.6 jit_solution(5087128734119464802)
XLA Ops:
  0.6 252.6 %arrow_solve.1 = (f32[2,384,128]{2,1,0:T(8,128)}, f32[384,128]{1,0:T(8,128)}) custom-call(f32[2,384,384]{2,1,0:T(8,128)} %trans.1, f32[2,384]{1,0:T(2,128)} %innov.1, f32[2,384]{1,0:T(2,128)} %observ.1, f32[2,384,384]{2,1,0:T(8,128)} %effects.1, f32[384]{0:T(512)} %prior.1, f32[2,384,128]{2,1,0:T(8,128)} %right.1, f32[384,128]{1,0:T(8,128)} %tip_right.1), custom_call_target="tpu_custom_call" | custom-call | tf_op jit(solution)/shard_map/arrow_solve/pallas_call | solution.py:559
  253.2 1.8 copy.11
  255.0 1.6 copy.12
